TPU v7x, 128 devices: a whole 4x4x4 slice. The times are simulated.
128 devices in a mesh: req: 16 (over x, z), mlp: 8 (over y, core).
Axes of the slice: x: 4, y: 4, z: 4, core: 2. Of those that a mesh axis runs over, the one named last changes fastest.
Arguments:
- patches: bfloat16 [15360, 4096], P('req'), may hold values from -6 to 6
- norm_gain: float32 [4096], replicated, may hold values from 0.25 to 1.75
- norm_bias: float32 [4096], replicated, may hold values from -3 to 3
- gate_weight: bfloat16 [4096, 8192], P(None, ('req', 'mlp')), may hold values from -0.09375 to 0.09375
- up_weight: bfloat16 [4096, 8192], P(None, ('req', 'mlp')), may hold values from -0.09375 to 0.09375
- down_weight: bfloat16 [4096, 8192], P(None, ('req', 'mlp')), may hold values from -0.0625 to 0.0625
- layer_scale: float32 [4096], replicated, may hold values from 0.25 to 2.5
- projection: bfloat16 [4, 4096, 4096], P(None, 'mlp', 'req'), may hold values from -0.046875 to 0.046875
- text_rows: bfloat16 [65536, 4096], P(('req', 'mlp')), may hold values from -6 to 6
- destination: int32 [3840], replicated, may hold values from -1 to 65535, as said below
Outputs:
- patch_out: bfloat16 [15360, 4096], P('req', 'mlp')
- streams: bfloat16 [65536, 4096], P(('req', 'mlp'))
Inputs may be any that keep to these rules, and one draw needn't show every extreme that they name: `destination`: values other than -1 are distinct positions; the positions landing in one piece of 512 consecutive positions (a stream holds 8 pieces) form one run of consecutive positions, at least one and at most 30 of them, and some piece receives exactly 30.
All inputs are finite; a program needn't handle non-finite values.
Results may differ from a plain program's by a relative error of at most 0.015.
Values may be sent and summed in bfloat16 or wider, within the bound.
No kernel may reach another device: no remote copies, remote signals or barrier semaphores. Data moves between devices by JAX's collectives and lax.ppermute only.
A program may use at most 128 MiB of HBM per device.

v0:
```python
import jax
import jax.numpy as jnp
from jax import lax
from jax.sharding import PartitionSpec as P


def layer_norm(values, norm_gain, norm_bias):
    row_mean = jnp.mean(values, axis=-1, keepdims=True)
    centred = values - row_mean
    variance = jnp.mean(centred * centred, axis=-1, keepdims=True)
    return centred * lax.rsqrt(variance + 1e-06) * norm_gain + norm_bias


def shards(
    patches,
    norm_gain,
    norm_bias,
    gate_weight,
    up_weight,
    down_weight,
    layer_scale,
    projection,
    text_rows,
    destination,
):
    req_count = lax.axis_size("req")
    mlp_count = lax.axis_size("mlp")
    req_index = lax.axis_index("req")
    mlp_index = lax.axis_index("mlp")
    rows_here, model_width = patches.shape
    feat_width = model_width // mlp_count
    inputs = patches.astype(jnp.float32)
    normed = layer_norm(inputs, norm_gain, norm_bias).astype(jnp.bfloat16)
    gate_act = jnp.dot(
        normed,
        lax.all_gather(gate_weight, "req", axis=1, tiled=True),
        preferred_element_type=jnp.float32,
    )
    up_act = jnp.dot(
        normed,
        lax.all_gather(up_weight, "req", axis=1, tiled=True),
        preferred_element_type=jnp.float32,
    )
    hidden = (jax.nn.silu(gate_act) * up_act).astype(jnp.bfloat16)
    ffn_local = lax.dot_general(
        hidden,
        lax.all_gather(down_weight, "req", axis=1, tiled=True),
        (((1,), (1,)), ((), ())),
        preferred_element_type=jnp.float32,
    )
    partial_value = lax.optimization_barrier(ffn_local.astype(jnp.bfloat16)).astype(jnp.float32)
    ffn_feats = lax.psum_scatter(
        partial_value.astype(jnp.bfloat16), "mlp", scatter_dimension=1, tiled=True
    ).astype(jnp.float32)
    scale_here = lax.dynamic_slice_in_dim(layer_scale, mlp_index * feat_width, feat_width)
    own_inputs = lax.dynamic_slice_in_dim(inputs, mlp_index * feat_width, feat_width, axis=1)
    patch_out = (own_inputs + scale_here * ffn_feats).astype(jnp.bfloat16)
    merged = patch_out.reshape(rows_here // 4, 4 * feat_width)
    weight_cols = projection.reshape(4 * feat_width, projection.shape[2])
    piece_rows = text_rows.shape[0]
    slot_count = destination.shape[0]
    bucket_count = req_count * mlp_count
    capacity = slot_count // bucket_count
    is_valid = destination >= 0
    piece_ids = jnp.where(is_valid, destination // piece_rows, -1)
    offsets = destination % piece_rows
    bucket_hit = piece_ids[:, None] == jnp.arange(bucket_count, dtype=jnp.int32)[None, :]
    first_off = jnp.min(jnp.where(bucket_hit, offsets[:, None], piece_rows), axis=0)
    counts = jnp.sum(bucket_hit.astype(jnp.int32), axis=0)
    slot_first = jnp.sum(jnp.where(bucket_hit, first_off[None, :], 0), axis=1)
    slot_rank = offsets - slot_first
    stream_ids = piece_ids // mlp_count
    piece_in = piece_ids % mlp_count
    rows_at = piece_in * (req_count * capacity) + stream_ids * capacity + slot_rank
    rows_at = jnp.where(is_valid, rows_at, bucket_count * capacity)
    sources = (
        jnp.full((bucket_count * capacity,), -1, jnp.int32)
        .at[rows_at]
        .set(jnp.arange(slot_count, dtype=jnp.int32), mode="drop")
    )
    every_row = lax.all_gather(merged, "req", axis=0, tiled=True)
    picked_rows = jnp.take(every_row, jnp.maximum(sources, 0), axis=0)
    picked_rows = jnp.where(sources[:, None] >= 0, picked_rows, jnp.zeros_like(picked_rows))
    summed = lax.psum_scatter(
        jnp.dot(picked_rows, weight_cols, preferred_element_type=jnp.float32).astype(jnp.bfloat16),
        "mlp",
        scatter_dimension=0,
        tiled=True,
    )
    arrived = lax.all_to_all(summed, "req", split_axis=0, concat_axis=1, tiled=True)
    bucket_here = req_index * mlp_count + mlp_index
    start_here = first_off[bucket_here]
    count_here = counts[bucket_here]
    positions = jnp.arange(piece_rows, dtype=jnp.int32) - start_here
    inside = (positions >= 0) & (positions < count_here)
    image_rows = jnp.take(arrived, jnp.clip(positions, 0, capacity - 1), axis=0)
    streams = jnp.where(inside[:, None], image_rows, text_rows)
    return (patch_out, streams)


def solution(mesh):
    return jax.shard_map(
        shards,
        mesh=mesh,
        in_specs=(
            P("req", None),
            P(),
            P(),
            P(None, ("req", "mlp")),
            P(None, ("req", "mlp")),
            P(None, ("req", "mlp")),
            P(),
            P(None, "mlp", "req"),
            P(("req", "mlp"), None),
            P(),
        ),
        out_specs=(P("req", "mlp"), P(("req", "mlp"), None)),
        check_vma=False,
    )
```

profile of v0, /device:TPU:0, one launch (start us, length us, event | category | flops | bytes accessed | tf_op | source)
XLA Modules:
  0.0 527.9 jit_solution(9855831558795438825)
XLA Ops:
  7.2 0.0 copy-start
  7.2 0.0 all-gather.5.cloned.1.call-start
  7.2 0.7 all-gather.5.cloned.1.call-update
  7.9 0.0 all-gather.7.cloned.1.call-start
  8.0 0.7 all-gather.7.cloned.1.call-update
  8.7 0.0 all-gather.9.cloned.1.call-start
  8.7 0.7 all-gather.9.cloned.1.call-update
  9.4 0.0 reduce-scatter.3.cloned.1.call-start
  9.4 0.0 copy-start.1
  9.5 0.0 copy-start.4
  9.5 0.0 copy-start.5
  9.5 4.5 convert_reduce_fusion
  14.0 1.0 copy-done.1
  14.9 2.2 multiply_reduce_fusion
  17.1 66.4 %all-gather.5.cloned.1.call-done = bf16[4096,1024]{0,1:T(8,128)(2,1)} async-done(((bf16[4096,64]{0,1:T(8,128)(2,1)}), bf16[4096,1024]{0,1:T(8,128)(2,1)}) %all-gather.5.cloned.1.call-update) | async-done | bytes 8388624 | tf_op jit(solution)/shard_map/all_gather | solution.py:36
  83.5 0.0 copy-done.4
  83.5 0.0 copy-done.5
  83.5 14.4 %fusion.31 = f32[960,1024]{1,0:T(8,128)} fusion(bf16[4096,1024]{0,1:T(8,128)(2,1)} %all-gather.5.cloned.1.call-done, bf16[960,4096]{1,0:T(8,128)(2,1)} %param.10, f32[4096]{0:T(1024)S(1)} %copy-done.4, f32[4096]{0:T(1024)S(1)} %copy-done.5, f32[960]{0:T(1024)S(1)} %add_rsqrt_fusion, f32[960]{0:T(1024)S(1)} %broadcast_multiply_fusion), kind=kOutput, calls=%fused_computation.68 | convolution fusion | flops 8076656640 | bytes 20225536 | tf_op jit(solution)/shard_map/dot_general | solution.py:34
  97.9 58.2 %all-gather.7.cloned.1.call-done = bf16[4096,1024]{0,1:T(8,128)(2,1)} async-done(((bf16[4096,64]{0,1:T(8,128)(2,1)}), bf16[4096,1024]{0,1:T(8,128)(2,1)}) %all-gather.7.cloned.1.call-update) | async-done | bytes 8388624 | tf_op jit(solution)/shard_map/all_gather | solution.py:41
  156.1 72.6 %all-gather.9.cloned.1.call-done = bf16[4096,1024]{0,1:T(8,128)(2,1)} async-done(((bf16[4096,64]{0,1:T(8,128)(2,1)}), bf16[4096,1024]{0,1:T(8,128)(2,1)}) %all-gather.9.cloned.1.call-update) | async-done | bytes 8388624 | tf_op jit(solution)/shard_map/all_gather | solution.py:47
  228.7 25.9 %convolution_convert_fusion = bf16[960,4096]{1,0:T(8,128)(2,1)} fusion(bf16[4096,1024]{0,1:T(8,128)(2,1)} %all-gather.9.cloned.1.call-done, f32[960,1024]{1,0:T(8,128)} %fusion.31, bf16[4096,1024]{0,1:T(8,128)(2,1)} %all-gather.7.cloned.1.call-done, bf16[960,4096]{1,0:T(8,128)(2,1)} %param.10, f32[4096]{0:T(1024)S(1)} %copy-done.4, f32[4096]{0:T(1024)S(1)} %copy-done.5, ...), kind=kOutput, calls=%fused_computation.13 | convolution fusion | flops 16139550720 | bytes 36478464 | tf_op jit(solution)/shard_map/dot_general | solution.py:45
  254.6 0.0 reduce-scatter.3.cloned.1.call-update
  254.6 0.0 all-gather.11.cloned.1.call-start
  254.7 0.0 copy-start.3
  254.7 11.3 %convert_element_type.26 = f32[960,4096]{1,0:T(8,128)} convert(bf16[960,4096]{1,0:T(8,128)(2,1)} %param.10) | non-fusion elementwise | flops 3932160 | bytes 23592960 | tf_op jit(solution)/shard_map/convert_element_type | solution.py:32
  266.0 0.8 dynamic_slice.13
  266.7 37.6 %reduce-scatter.3.cloned.1.call-done = bf16[960,512]{1,0:T(8,128)(2,1)} async-done(((bf16[960,4096]{1,0:T(8,128)(2,1)}), bf16[960,512]{1,0:T(8,128)(2,1)}) %reduce-scatter.3.cloned.1.call-update) | async-done | bytes 983056 | tf_op jit(solution)/shard_map/reduce_scatter | solution.py:52
  304.3 2.2 add_convert_fusion.1
  306.5 0.0 copy-start.2
  306.5 1.5 reshape.67
  308.0 0.0 all-gather.11.cloned.1.call-update
  308.0 0.0 reduce-scatter.5.cloned.1.call-start
  308.1 0.0 copy-done.3
  308.1 2.5 select_reduce_fusion.1
  310.6 2.4 convert_reduce_fusion.1
  313.1 14.6 %scatter_custom_fusion = s32[3840]{0:T(1024)S(1)} fusion(s32[3840]{0:T(1024)S(1)} %compare_select_fusion, s32[3840]{0:T(1024)S(1)} %iota.16, s32[]{:T(128)} %constant.104.clone.1), kind=kCustom, calls=%fused_computation.51 | custom fusion | bytes 15364 | tf_op jit(solution)/shard_map/scatter | solution.py:79
  327.7 86.2 %all-gather.11.cloned.1.call-done = bf16[3840,2048]{1,0:T(8,128)(2,1)} async-done(((bf16[240,2048]{1,0:T(8,128)(2,1)}), bf16[3840,2048]{1,0:T(8,128)(2,1)}) %all-gather.11.cloned.1.call-update) | async-done | bytes 15728656 | tf_op jit(solution)/shard_map/all_gather | solution.py:81
  413.9 37.0 %gather_fusion = bf16[3840,2048]{1,0:T(8,128)(2,1)} fusion(bf16[3840,2048]{1,0:T(8,128)(2,1)} %all-gather.11.cloned.1.call-done, s32[4096]{0:T(1024)S(1)} %pad_clamp_fusion), kind=kCustom, calls=%fused_computation | custom fusion | bytes 31472640 | tf_op jit(solution)/shard_map/jit(_take)/gather | solution.py:82
  450.9 0.0 copy-done.2
  450.9 0.0 copy-done
  450.9 9.9 %fusion.7 = bf16[3840,256]{1,0:T(8,128)(2,1)} fusion(bf16[2048,256]{1,0:T(8,128)(2,1)S(1)} %bitcast.13, bf16[3840,2048]{1,0:T(8,128)(2,1)} %gather_fusion, pred[3840]{0:T(1024)(128)(4,1)S(1)} %get-tuple-element.5, pred[3840]{0:T(1024)(128)(4,1)S(1)} %get-tuple-element.4), kind=kOutput, calls=%fused_computation.14 | convolution fusion | flops 4043243520 | bytes 18750976 | tf_op jit(solution)/shard_map/dot_general | solution.py:85
  460.8 0.0 reduce-scatter.5.cloned.1.call-update
  460.8 0.6 dynamic_slice.14
  461.4 0.6 dynamic_slice.15
  462.1 31.9 %reduce-scatter.5.cloned.1.call-done = bf16[480,256]{1,0:T(8,128)(2,1)} async-done(((bf16[3840,256]{1,0:T(8,128)(2,1)}), bf16[480,256]{1,0:T(8,128)(2,1)}) %reduce-scatter.5.cloned.1.call-update) | async-done | bytes 245776 | tf_op jit(solution)/shard_map/reduce_scatter | solution.py:84
  494.0 1.7 all_to_all.14
  495.7 6.9 %all-to-all-start = ((bf16[16,30,256]{2,1,0:T(8,128)(2,1)}), bf16[16,30,256]{2,1,0:T(8,128)(2,1)S(1)}, u32[]{:S(2)}, u32[]{:S(2)}) async-start(bf16[16,30,256]{2,1,0:T(8,128)(2,1)} %all_to_all.14), calls=%async_computation.2 | async-start | bytes 524288 | tf_op jit(solution)/shard_map/all_to_all | solution.py:90
  502.6 1.3 fusion.27
  503.9 0.6 compare_select_fusion.1
  504.6 6.5 %all-to-all-done = bf16[16,30,256]{2,1,0:T(8,128)(2,1)S(1)} async-done(((bf16[16,30,256]{2,1,0:T(8,128)(2,1)}), bf16[16,30,256]{2,1,0:T(8,128)(2,1)S(1)}, u32[]{:S(2)}, u32[]{:S(2)}) %all-to-all-start) | async-done | bytes 245792 | tf_op jit(solution)/shard_map/all_to_all | solution.py:90
  511.1 0.1 copy.14
  511.3 0.1 copy.15
  511.4 4.4 gather_fusion.1
  515.7 5.3 select_select_fusion
  (10 shorter events, 0.1 us)
Async XLA Ops:
  7.2 443.7 %copy-start = (bf16[4,512,256]{2,1,0:T(8,128)(2,1)S(1)}, bf16[4,512,256]{2,1,0:T(8,128)(2,1)}, u32[]{:S(2)}) copy-start(bf16[4,512,256]{2,1,0:T(8,128)(2,1)} %param.17) | copy-start | bytes 3145732
  7.2 76.3 %all-gather.5.cloned.1.call-start = ((), (), s32[]{:S(2)}) async-start(), calls=%async_computation.3 | async-start | bytes 8912896 | tf_op jit(solution)/shard_map/all_gather | solution.py:36
  7.9 148.2 %all-gather.7.cloned.1.call-start = ((), (), s32[]{:S(2)}) async-start(), calls=%async_computation.4 | async-start | bytes 8912896 | tf_op jit(solution)/shard_map/all_gather | solution.py:41
  8.7 220.1 %all-gather.9.cloned.1.call-start = ((), (), s32[]{:S(2)}) async-start(), calls=%async_computation.5 | async-start | bytes 8912896 | tf_op jit(solution)/shard_map/all_gather | solution.py:47
  9.4 294.9 %reduce-scatter.3.cloned.1.call-start = ((), (), s32[]{:S(2)}) async-start(), calls=%async_computation.6 | async-start | bytes 8847360 | tf_op jit(solution)/shard_map/reduce_scatter | solution.py:52
  9.4 5.5 %copy-start.1 = (bf16[960,4096]{1,0:T(8,128)(2,1)S(1)}, bf16[960,4096]{1,0:T(8,128)(2,1)}, u32[]{:S(2)}) copy-start(bf16[960,4096]{1,0:T(8,128)(2,1)} %param.10) | copy-start | bytes 23592964
  9.5 74.1 %copy-start.4 = (f32[4096]{0:T(1024)S(1)}, f32[4096]{0:T(1024)}, u32[]{:S(2)}) copy-start(f32[4096]{0:T(1024)} %param.12) | copy-start | bytes 49156
  9.5 74.1 %copy-start.5 = (f32[4096]{0:T(1024)S(1)}, f32[4096]{0:T(1024)}, u32[]{:S(2)}) copy-start(f32[4096]{0:T(1024)} %param.11) | copy-start | bytes 49156
  254.6 159.3 %all-gather.11.cloned.1.call-start = ((), (), s32[]{:S(2)}) async-start(), calls=%async_computation.7 | async-start | bytes 16711680 | tf_op jit(solution)/shard_map/all_gather | solution.py:81
  254.7 53.4 %copy-start.3 = (s32[3840]{0:T(1024)S(1)}, s32[3840]{0:T(1024)}, u32[]{:S(2)}) copy-start(s32[3840]{0:T(1024)} %param.19) | copy-start | bytes 46084
  306.5 144.4 %copy-start.2 = (bf16[960,512]{1,0:T(8,128)(2,1)}, bf16[960,512]{1,0:T(8,128)(2,1)S(1)}, u32[]{:S(2)}) copy-start(bf16[960,512]{1,0:T(8,128)(2,1)S(1)} %add_convert_fusion.1) | copy-start | bytes 2949124
  308.0 186.0 %reduce-scatter.5.cloned.1.call-start = ((), (), s32[]{:S(2)}) async-start(), calls=%async_computation.8 | async-start | bytes 2211840 | tf_op jit(solution)/shard_map/reduce_scatter | solution.py:84
  495.7 15.4 %all-to-all-start = ((bf16[16,30,256]{2,1,0:T(8,128)(2,1)}), bf16[16,30,256]{2,1,0:T(8,128)(2,1)S(1)}, u32[]{:S(2)}, u32[]{:S(2)}) async-start(bf16[16,30,256]{2,1,0:T(8,128)(2,1)} %all_to_all.14), calls=%async_computation.2 | async-start | bytes 524288 | tf_op jit(solution)/shard_map/all_to_all | solution.py:90
Sparse Core Ops, SparseCore 0:
  10.2 73.3 all-gather.4
  85.7 70.4 all-gather.6
  158.3 70.4 all-gather.8
  254.7 49.5 reduce-scatter.2
  308.2 105.6 all-gather.10
  460.9 33.0 reduce-scatter.4
where the time goes:
time: 528 us
  waiting for transfers between devices  362 us (69%)
  local copies, waits for them, and re-layouts  62.5 us (12%)
  matrix products  50.1 us (9%)
  other arithmetic  32.3 us (6%)
  between operations  14.3 us (3%)
  starting transfers between devices  7.14 us (1%)
    all_gather x1, waiting for transfers between devices, shards(): every_row = lax.all_gather(merged, 'req', axis=0, tiled=True)  86.2 us
    all_gather x1, waiting for transfers between devices, shards(): lax.all_gather(down_weight, 'req', axis=1, tiled=True)  72.6 us
    all_gather x1, waiting for transfers between devices, shards(): lax.all_gather(gate_weight, 'req', axis=1, tiled=True)  66.4 us
    all_gather x1, waiting for transfers between devices, shards(): lax.all_gather(up_weight, 'req', axis=1, tiled=True)  58.2 us
    reduce_scatter x1, waiting for transfers between devices, shards(): lax.psum_scatter(partial_value.astype(jnp.bfloat16), 'mlp', scatter_dimen...  37.6 us
    gather x1, local copies, waits for them, and re-layouts, shards(): picked_rows = jnp.take(every_row, jnp.maximum(sources, 0), axis=0)  37 us
    reduce_scatter x1, waiting for transfers between devices, shards(): lax.psum_scatter(jnp.dot(picked_rows, weight_cols, preferred_element_type...  31.9 us
    dot_general x1, matrix products, shards(): lax.dot_general(hidden, lax.all_gather(down_weight, 'req', axis=1, tiled=...  25.9 us
  transfers between devices with their start and end apart: 7, of which 7 were waited for; matrix products, arithmetic and copies ran while one was open for 11% of the time, Pallas kernels for 0%

commit v1 on v0

--- a/solution.py
+++ b/solution.py
@@ -87,7 +87,10 @@
         scatter_dimension=0,
         tiled=True,
     )
-    arrived = lax.all_to_all(summed, "req", split_axis=0, concat_axis=1, tiled=True)
+    arrived = jnp.concatenate(
+        lax.all_to_all(jnp.stack(jnp.split(summed, lax.axis_size("req"), axis=0)), "req", 0, 0),
+        axis=1,
+    )
     bucket_here = req_index * mlp_count + mlp_index
     start_here = first_off[bucket_here]
     count_here = counts[bucket_here]

time: 528 us -> 549 us (1.040)
  local copies, waits for them, and re-layouts: 62.5 us -> 82.1 us
    unnamed x14 -> x29, local copies, waits for them, and re-layouts: 1.09 us -> 21.1 us
  transfers between devices with their start and end apart: 7 -> 7, of which waited for: 7 -> 7; matrix products, arithmetic and copies ran while one was open for 11% -> 10% of each run, Pallas kernels for 0% -> 0%
where the time goes in v1:
time: 549 us; the launch traced here: 547 us
  waiting for transfers between devices  362 us (66%)
  local copies, waits for them, and re-layouts  82.1 us (15%)
  matrix products  50.1 us (9%)
  other arithmetic  32.3 us (6%)
  between operations  14.3 us (3%)
  starting transfers between devices  7.14 us (1%)
    all_gather x1, waiting for transfers between devices, shards(): every_row = lax.all_gather(merged, 'req', axis=0, tiled=True)  86.2 us
    all_gather x1, waiting for transfers between devices, shards(): lax.all_gather(down_weight, 'req', axis=1, tiled=True)  72.6 us
    all_gather x1, waiting for transfers between devices, shards(): lax.all_gather(gate_weight, 'req', axis=1, tiled=True)  66.4 us
    all_gather x1, waiting for transfers between devices, shards(): lax.all_gather(up_weight, 'req', axis=1, tiled=True)  58.2 us
    reduce_scatter x1, waiting for transfers between devices, shards(): lax.psum_scatter(partial_value.astype(jnp.bfloat16), 'mlp', scatter_dimen...  37.6 us
    gather x1, local copies, waits for them, and re-layouts, shards(): picked_rows = jnp.take(every_row, jnp.maximum(sources, 0), axis=0)  37 us
    reduce_scatter x1, waiting for transfers between devices, shards(): lax.psum_scatter(jnp.dot(picked_rows, weight_cols, preferred_element_type...  31.9 us
    dot_general x1, matrix products, shards(): lax.dot_general(hidden, lax.all_gather(down_weight, 'req', axis=1, tiled=...  25.9 us
  transfers between devices with their start and end apart: 7, of which 7 were waited for; matrix products, arithmetic and copies ran while one was open for 10% of the time, Pallas kernels for 0%

profile of v1, /device:TPU:0, one launch (start us, length us, event | category | flops | bytes accessed | tf_op | source)
XLA Modules:
  0.0 547.5 jit_solution(13415283467542613330)
XLA Ops:
  7.2 0.0 copy-start
  7.2 0.0 all-gather.5.cloned.1.call-start
  7.2 0.7 all-gather.5.cloned.1.call-update
  7.9 0.0 all-gather.7.cloned.1.call-start
  8.0 0.7 all-gather.7.cloned.1.call-update
  8.7 0.0 all-gather.9.cloned.1.call-start
  8.7 0.7 all-gather.9.cloned.1.call-update
  9.4 0.0 reduce-scatter.3.cloned.1.call-start
  9.4 0.0 copy-start.1
  9.5 0.0 copy-start.4
  9.5 4.5 convert_reduce_fusion
  14.0 1.0 copy-done.1
  14.9 2.2 multiply_reduce_fusion
  17.1 66.4 %all-gather.5.cloned.1.call-done = bf16[4096,1024]{0,1:T(8,128)(2,1)} async-done(((bf16[4096,64]{0,1:T(8,128)(2,1)}), bf16[4096,1024]{0,1:T(8,128)(2,1)}) %all-gather.5.cloned.1.call-update) | async-done | bytes 8388624 | tf_op jit(solution)/shard_map/all_gather | solution.py:36
  83.5 14.4 %fusion.31 = f32[960,1024]{1,0:T(8,128)} fusion(bf16[4096,1024]{0,1:T(8,128)(2,1)} %all-gather.5.cloned.1.call-done, bf16[960,4096]{1,0:T(8,128)(2,1)} %param.10, f32[4096]{0:T(1024)S(1)} %copy-done.4, f32[4096]{0:T(1024)S(1)} %copy-done.5, f32[960]{0:T(1024)S(1)} %add_rsqrt_fusion, f32[960]{0:T(1024)S(1)} %broadcast_multiply_fusion), kind=kOutput, calls=%fused_computation.100 | convolution fusion | flops 8076656640 | bytes 20225536 | tf_op jit(solution)/shard_map/dot_general | solution.py:34
  97.9 58.2 %all-gather.7.cloned.1.call-done = bf16[4096,1024]{0,1:T(8,128)(2,1)} async-done(((bf16[4096,64]{0,1:T(8,128)(2,1)}), bf16[4096,1024]{0,1:T(8,128)(2,1)}) %all-gather.7.cloned.1.call-update) | async-done | bytes 8388624 | tf_op jit(solution)/shard_map/all_gather | solution.py:41
  156.1 72.6 %all-gather.9.cloned.1.call-done = bf16[4096,1024]{0,1:T(8,128)(2,1)} async-done(((bf16[4096,64]{0,1:T(8,128)(2,1)}), bf16[4096,1024]{0,1:T(8,128)(2,1)}) %all-gather.9.cloned.1.call-update) | async-done | bytes 8388624 | tf_op jit(solution)/shard_map/all_gather | solution.py:47
  228.7 25.9 %convolution_convert_fusion = bf16[960,4096]{1,0:T(8,128)(2,1)} fusion(bf16[4096,1024]{0,1:T(8,128)(2,1)} %all-gather.9.cloned.1.call-done, f32[960,1024]{1,0:T(8,128)} %fusion.31, bf16[4096,1024]{0,1:T(8,128)(2,1)} %all-gather.7.cloned.1.call-done, bf16[960,4096]{1,0:T(8,128)(2,1)} %param.10, f32[4096]{0:T(1024)S(1)} %copy-done.4, f32[4096]{0:T(1024)S(1)} %copy-done.5, ...), kind=kOutput, calls=%fused_computation.13 | convolution fusion | flops 16139550720 | bytes 36478464 | tf_op jit(solution)/shard_map/dot_general | solution.py:45
  254.6 0.0 reduce-scatter.3.cloned.1.call-update
  254.6 0.0 all-gather.11.cloned.1.call-start
  254.7 0.0 copy-start.3
  254.7 11.3 %convert_element_type.26 = f32[960,4096]{1,0:T(8,128)} convert(bf16[960,4096]{1,0:T(8,128)(2,1)} %param.10) | non-fusion elementwise | flops 3932160 | bytes 23592960 | tf_op jit(solution)/shard_map/convert_element_type | solution.py:32
  266.0 0.8 dynamic_slice.13
  266.7 37.6 %reduce-scatter.3.cloned.1.call-done = bf16[960,512]{1,0:T(8,128)(2,1)} async-done(((bf16[960,4096]{1,0:T(8,128)(2,1)}), bf16[960,512]{1,0:T(8,128)(2,1)}) %reduce-scatter.3.cloned.1.call-update) | async-done | bytes 983056 | tf_op jit(solution)/shard_map/reduce_scatter | solution.py:52
  304.3 2.2 add_convert_fusion.1
  306.5 0.0 copy-start.2
  306.5 1.5 reshape.70
  308.0 0.0 all-gather.11.cloned.1.call-update
  308.0 0.0 reduce-scatter.5.cloned.1.call-start
  308.1 2.5 select_reduce_fusion.1
  310.6 2.4 convert_reduce_fusion.1
  313.1 14.6 %scatter_custom_fusion = s32[3840]{0:T(1024)S(1)} fusion(s32[3840]{0:T(1024)S(1)} %compare_select_fusion, s32[3840]{0:T(1024)S(1)} %iota.16, s32[]{:T(128)} %constant.104.clone.1), kind=kCustom, calls=%fused_computation.83 | custom fusion | bytes 15364 | tf_op jit(solution)/shard_map/scatter | solution.py:79
  327.7 86.2 %all-gather.11.cloned.1.call-done = bf16[3840,2048]{1,0:T(8,128)(2,1)} async-done(((bf16[240,2048]{1,0:T(8,128)(2,1)}), bf16[3840,2048]{1,0:T(8,128)(2,1)}) %all-gather.11.cloned.1.call-update) | async-done | bytes 15728656 | tf_op jit(solution)/shard_map/all_gather | solution.py:81
  413.9 37.0 %gather_fusion = bf16[3840,2048]{1,0:T(8,128)(2,1)} fusion(bf16[3840,2048]{1,0:T(8,128)(2,1)} %all-gather.11.cloned.1.call-done, s32[4096]{0:T(1024)S(1)} %pad_clamp_fusion), kind=kCustom, calls=%fused_computation | custom fusion | bytes 31472640 | tf_op jit(solution)/shard_map/jit(_take)/gather | solution.py:82
  450.9 0.0 copy-done.2
  450.9 9.9 %fusion.7 = bf16[3840,256]{1,0:T(8,128)(2,1)} fusion(bf16[2048,256]{1,0:T(8,128)(2,1)S(1)} %bitcast.77, bf16[3840,2048]{1,0:T(8,128)(2,1)} %gather_fusion, pred[3840]{0:T(1024)(128)(4,1)S(1)} %get-tuple-element.5, pred[3840]{0:T(1024)(128)(4,1)S(1)} %get-tuple-element.4), kind=kOutput, calls=%fused_computation.14 | convolution fusion | flops 4043243520 | bytes 18750976 | tf_op jit(solution)/shard_map/dot_general | solution.py:85
  460.8 0.0 reduce-scatter.5.cloned.1.call-update
  460.8 0.6 dynamic_slice.14
  461.4 0.6 dynamic_slice.15
  462.1 31.9 %reduce-scatter.5.cloned.1.call-done = bf16[480,256]{1,0:T(8,128)(2,1)} async-done(((bf16[3840,256]{1,0:T(8,128)(2,1)}), bf16[480,256]{1,0:T(8,128)(2,1)}) %reduce-scatter.5.cloned.1.call-update) | async-done | bytes 245776 | tf_op jit(solution)/shard_map/reduce_scatter | solution.py:84
  494.0 1.3 constant_dynamic-update-slice_fusion.15
  495.3 1.3 constant_dynamic-update-slice_fusion.14
  496.7 1.3 constant_dynamic-update-slice_fusion.13
  498.0 1.3 constant_dynamic-update-slice_fusion.12
  499.3 1.3 constant_dynamic-update-slice_fusion.11
  500.7 1.3 constant_dynamic-update-slice_fusion.10
  502.0 1.3 constant_dynamic-update-slice_fusion.9
  503.3 1.3 constant_dynamic-update-slice_fusion.8
  504.7 1.3 constant_dynamic-update-slice_fusion.7
  506.0 1.3 constant_dynamic-update-slice_fusion.6
  507.3 1.3 constant_dynamic-update-slice_fusion.5
  508.7 1.3 constant_dynamic-update-slice_fusion.4
  510.0 1.3 constant_dynamic-update-slice_fusion.3
  511.3 1.3 constant_dynamic-update-slice_fusion.2
  512.7 1.3 constant_dynamic-update-slice_fusion.1
  514.0 1.3 constant_dynamic-update-slice_fusion
  515.3 6.9 %all-to-all-start = ((bf16[16,30,256]{2,1,0:T(8,128)(2,1)}), bf16[16,30,256]{2,1,0:T(8,128)(2,1)S(1)}, u32[]{:S(2)}, u32[]{:S(2)}) async-start(bf16[16,30,256]{2,1,0:T(8,128)(2,1)} %constant_dynamic-update-slice_fusion), calls=%async_computation.2 | async-start | bytes 524288 | tf_op jit(solution)/shard_map/all_to_all | solution.py:91
  522.3 1.3 fusion.27
  523.5 0.6 compare_select_fusion.1
  524.2 6.5 %all-to-all-done = bf16[16,30,256]{2,1,0:T(8,128)(2,1)S(1)} async-done(((bf16[16,30,256]{2,1,0:T(8,128)(2,1)}), bf16[16,30,256]{2,1,0:T(8,128)(2,1)S(1)}, u32[]{:S(2)}, u32[]{:S(2)}) %all-to-all-start) | async-done | bytes 245792 | tf_op jit(solution)/shard_map/all_to_all | solution.py:91
  530.7 0.1 copy.13
  530.9 0.1 copy.14
  531.0 4.4 gather_fusion.1
  535.4 5.3 select_select_fusion
  (15 shorter events, 0.1 us)
Async XLA Ops:
  7.2 443.7 %copy-start = (bf16[4,512,256]{2,1,0:T(8,128)(2,1)S(1)}, bf16[4,512,256]{2,1,0:T(8,128)(2,1)}, u32[]{:S(2)}) copy-start(bf16[4,512,256]{2,1,0:T(8,128)(2,1)} %param.17) | copy-start | bytes 3145732
  7.2 76.3 %all-gather.5.cloned.1.call-start = ((), (), s32[]{:S(2)}) async-start(), calls=%async_computation.3 | async-start | bytes 8912896 | tf_op jit(solution)/shard_map/all_gather | solution.py:36
  7.9 148.2 %all-gather.7.cloned.1.call-start = ((), (), s32[]{:S(2)}) async-start(), calls=%async_computation.4 | async-start | bytes 8912896 | tf_op jit(solution)/shard_map/all_gather | solution.py:41
  8.7 220.1 %all-gather.9.cloned.1.call-start = ((), (), s32[]{:S(2)}) async-start(), calls=%async_computation.5 | async-start | bytes 8912896 | tf_op jit(solution)/shard_map/all_gather | solution.py:47
  9.4 294.9 %reduce-scatter.3.cloned.1.call-start = ((), (), s32[]{:S(2)}) async-start(), calls=%async_computation.6 | async-start | bytes 8847360 | tf_op jit(solution)/shard_map/reduce_scatter | solution.py:52
  9.4 5.5 copy-start.1
  9.5 74.1 %copy-start.4 = (f32[4096]{0:T(1024)S(1)}, f32[4096]{0:T(1024)}, u32[]{:S(2)}) copy-start(f32[4096]{0:T(1024)} %param.12) | copy-start | bytes 49156
  9.5 74.1 %copy-start.5 = (f32[4096]{0:T(1024)S(1)}, f32[4096]{0:T(1024)}, u32[]{:S(2)}) copy-start(f32[4096]{0:T(1024)} %param.11) | copy-start | bytes 49156
  254.6 159.3 %all-gather.11.cloned.1.call-start = ((), (), s32[]{:S(2)}) async-start(), calls=%async_computation.7 | async-start | bytes 16711680 | tf_op jit(solution)/shard_map/all_gather | solution.py:81
  254.7 53.4 %copy-start.3 = (s32[3840]{0:T(1024)S(1)}, s32[3840]{0:T(1024)}, u32[]{:S(2)}) copy-start(s32[3840]{0:T(1024)} %param.19) | copy-start | bytes 46084
  306.5 144.4 %copy-start.2 = (bf16[960,512]{1,0:T(8,128)(2,1)}, bf16[960,512]{1,0:T(8,128)(2,1)S(1)}, u32[]{:S(2)}) copy-start(bf16[960,512]{1,0:T(8,128)(2,1)S(1)} %add_convert_fusion.1) | copy-start | bytes 2949124
  308.0 186.0 %reduce-scatter.5.cloned.1.call-start = ((), (), s32[]{:S(2)}) async-start(), calls=%async_computation.8 | async-start | bytes 2211840 | tf_op jit(solution)/shard_map/reduce_scatter | solution.py:84
  515.3 15.4 %all-to-all-start = ((bf16[16,30,256]{2,1,0:T(8,128)(2,1)}), bf16[16,30,256]{2,1,0:T(8,128)(2,1)S(1)}, u32[]{:S(2)}, u32[]{:S(2)}) async-start(bf16[16,30,256]{2,1,0:T(8,128)(2,1)} %constant_dynamic-update-slice_fusion), calls=%async_computation.2 | async-start | bytes 524288 | tf_op jit(solution)/shard_map/all_to_all | solution.py:91
Sparse Core Ops, SparseCore 0:
  10.2 73.3 all-gather.4
  85.7 70.4 all-gather.6
  158.3 70.4 all-gather.8
  254.7 49.5 reduce-scatter.2
  308.2 105.6 all-gather.10
  460.9 33.0 reduce-scatter.4
